TPU v7x, 512 devices: a whole 4x8x8 slice. The times are simulated.
512 devices in a mesh: rows: 64 (over x, y, core), cols: 8 (over z).
Axes of the slice: x: 4, y: 8, z: 8, core: 2. Of those that a mesh axis runs over, the one named last changes fastest.
Arguments:
- eigvecs: float32 [65536, 2048], P(('rows', 'cols')), may hold values from -6 to 6
- panels: float32 [8, 65536, 256], P('cols', 'rows'), may hold values from -0.375 to 0.375
- tfactors: float32 [2, 256, 256], replicated, may hold values from -0.03125 to 0.03125
- owners: int32 [2], replicated, may hold values from 0 to 7, as said below
Outputs:
- backvecs: float32 [65536, 2048], P('rows', 'cols')
Inputs may be any that keep to these rules, and one draw needn't show every extreme that they name: `owners`: the entries are distinct slots, among them 0 and 7.
All inputs are finite; a program needn't handle non-finite values.
Results may differ from a plain program's by a relative error of at most 0.00011.
Values sent between devices are 32-bit elements; how exact they have to be, the bound alone decides.
No kernel may reach another device: no remote copies, remote signals or barrier semaphores. Data moves between devices by JAX's collectives and lax.ppermute only.
A program may use at most 64 MiB of HBM per device.

v0:
```python
import jax
import jax.numpy as jnp
from jax import lax
from jax.sharding import PartitionSpec as P


def broadcast(x, axis, root):
    mine = lax.axis_index(axis) == root
    return lax.psum(jnp.where(mine, x, jnp.zeros_like(x)), axis)


def matmul(left, right):
    return jnp.dot(left, right, precision=lax.Precision.HIGHEST, preferred_element_type=jnp.float32)


def per_device(eigvecs, panels, tfactors, owners):
    tiles = lax.all_to_all(eigvecs, "cols", split_axis=1, concat_axis=0, tiled=True)
    count = tfactors.shape[0]
    local = panels[0]
    vectors = []
    for index in range(count):
        vectors.append(broadcast(local, "cols", owners[index]))
    factors = [jnp.triu(tfactors[index]) for index in range(count)]
    result = tiles
    for index in range(count):
        proj = lax.psum(matmul(vectors[index].T, result), "rows")
        coeff = matmul(factors[index], proj)
        result = result - matmul(vectors[index], coeff)
    return result


def solution(mesh):
    placed = (P(("rows", "cols"), None), P("cols", "rows", None), P(), P())
    return jax.shard_map(
        per_device, mesh=mesh, in_specs=placed, out_specs=P("rows", "cols"), check_vma=False
    )
```

profile of v0, /device:TPU:1, one launch (start us, length us, event | category | flops | bytes accessed | tf_op | source)
XLA Modules:
  0.0 508.5 jit_solution(2413982245606252921)
XLA Ops:
  6.5 0.0 all-reduce.9.cloned.1.call-start
  6.5 0.0 copy-start.4
  6.5 0.7 copy-done.4
  7.2 0.6 fusion.10
  9.1 2.7 select_bitcast_fusion
  11.7 0.0 copy-start.1
  11.8 0.0 all-reduce.9.cloned.1.call-update
  11.8 0.0 all-reduce.5.cloned.1.call-start
  11.8 1.1 copy-done.1
  13.0 0.1 copy.8
  13.1 45.1 %all_to_all.19 = f32[128,8,256]{2,0,1:T(8,128)S(1)} all-to-all(f32[128,8,256]{2,0,1:T(8,128)S(1)} %bitcast.31), channel_id=1, replica_groups=mesh['rows'=64,'cols'=8] {'cols'}, dimensions={1} | all-to-all | bytes 2097152 | tf_op jit(solution)/shard_map/all_to_all | solution.py:17
  58.2 58.0 %all-reduce.9.cloned.1.call-done = (f32[1024,256]{1,0:T(8,128)}, f32[1024,256]{1,0:T(8,128)}) async-done(((f32[1024,256]{1,0:T(8,128)}, f32[1024,256]{1,0:T(8,128)}), (f32[1024,256]{1,0:T(8,128)}, f32[1024,256]{1,0:T(8,128)})) %all-reduce.9.cloned.1.call-update) | async-done | bytes 2097168 | tf_op jit(solution)/shard_map/psum | solution.py:9
  116.2 0.0 copy-start.2
  116.2 3.8 fusion.11
  120.0 0.0 all-reduce.5.cloned.1.call-update
  120.0 0.0 all-reduce.7.cloned.1.call-start
  120.0 188.2 %all-reduce.5.cloned.1.call-done = f32[256,256]{1,0:T(8,128)} async-done(((f32[256,256]{1,0:T(8,128)}), f32[256,256]{1,0:T(8,128)}) %all-reduce.5.cloned.1.call-update) | async-done | bytes 262160 | tf_op jit(solution)/shard_map/psum | solution.py:26
  308.2 0.0 copy-done.2
  308.2 1.4 fusion.1
  309.6 0.0 copy-start
  309.6 2.3 convolution_subtract_fusion.1
  311.9 0.0 copy-done
  311.9 0.0 copy-start.3
  312.0 2.5 fusion.12
  314.5 0.0 all-reduce.7.cloned.1.call-update
  314.5 184.1 %all-reduce.7.cloned.1.call-done = f32[256,256]{1,0:T(8,128)} async-done(((f32[256,256]{1,0:T(8,128)}), f32[256,256]{1,0:T(8,128)}) %all-reduce.7.cloned.1.call-update) | async-done | bytes 262160 | tf_op jit(solution)/shard_map/psum | solution.py:26
  498.6 0.0 copy-done.3
  498.6 1.4 fusion
  500.0 2.0 convolution_subtract_fusion
  (1 shorter events, 0.0 us)
Async XLA Ops:
  6.5 109.6 %all-reduce.9.cloned.1.call-start = ((), (), s32[]{:S(2)}) async-start(), calls=%async_computation.3 | async-start | bytes 4194304 | tf_op jit(solution)/shard_map/psum | solution.py:9
  6.5 0.7 copy-start.4
  11.7 1.2 copy-start.1
  11.8 296.5 %all-reduce.5.cloned.1.call-start = ((), (), s32[]{:S(2)}) async-start(), calls=%async_computation.1 | async-start | bytes 524288 | tf_op jit(solution)/shard_map/psum | solution.py:26
  116.2 192.1 %copy-start.2 = (f32[2,256,256]{2,1,0:T(8,128)S(1)}, f32[2,256,256]{2,1,0:T(8,128)}, u32[]{:S(2)}) copy-start(f32[2,256,256]{2,1,0:T(8,128)} %param.6) | copy-start | bytes 1572868
  120.0 378.7 %all-reduce.7.cloned.1.call-start = ((), (), s32[]{:S(2)}) async-start(), calls=%async_computation.2 | async-start | bytes 524288 | tf_op jit(solution)/shard_map/psum | solution.py:26
  309.6 2.3 copy-start
  311.9 186.7 %copy-start.3 = (f32[2,256,256]{2,1,0:T(8,128)S(1)}, f32[2,256,256]{2,1,0:T(8,128)}, u32[]{:S(2)}) copy-start(f32[2,256,256]{2,1,0:T(8,128)} %param.6) | copy-start | bytes 1572868
Sparse Core Ops, SparseCore 0:
  11.9 104.2 all-reduce.8
  120.1 188.0 all-reduce.4
  314.6 183.9 all-reduce.6
where the time goes:
time: 509 us
  waiting for transfers between devices  430 us (84%)
  blocking collectives  45.1 us (9%)
  between operations  14.5 us (3%)
  matrix products  13.3 us (3%)
    psum x2, waiting for transfers between devices, per_device(): proj = lax.psum(matmul(vectors[index].T, result), 'rows')  372 us
    psum x1, waiting for transfers between devices, broadcast(): return lax.psum(jnp.where(mine, x, jnp.zeros_like(x)), axis)  58 us
    all_to_all x1, blocking collectives, per_device(): lax.all_to_all(eigvecs, 'cols', split_axis=1, concat_axis=0, tiled=True)  45.1 us
    dot_general x6, matrix products, matmul(): jnp.dot(left, right, precision=lax.Precision.HIGHEST, preferred_element_t...  13.3 us
  transfers between devices with their start and end apart: 3, of which 3 were waited for; matrix products, arithmetic and copies ran while one was open for 0% of the time, Pallas kernels for 0%

commit v1 on v0

v1 whole, which is shorter than its diff:
```python
import jax
import jax.numpy as jnp
from jax import lax
from jax.sharding import Mesh, PartitionSpec as P

HIGHEST = lax.Precision.HIGHEST
PLANE = ("x", "y")


def dot(left, right, dims):
    return lax.dot_general(left, right, (dims, ((), ())), precision=HIGHEST, preferred_element_type=jnp.float32)


def tn(left, right):
    return dot(left, right, ((0,), (0,)))


def nn(left, right):
    return dot(left, right, ((1,), (0,)))


def gather_panels(local, owners):
    rows = local.shape[0]
    quarter = rows // 4
    slot = lax.axis_index("z")
    last = lax.axis_size("z") - 1
    half = (last + 1) // 2
    mine = lax.dynamic_slice_in_dim(local, jnp.where(slot == last, rows - quarter, 0), quarter)
    chunk = mine
    for step in range(1, half):
        start = jnp.where(slot == last, (half - 1 - step) * quarter, step * quarter)
        piece = lax.dynamic_slice_in_dim(local, start, quarter)
        piece = lax.ppermute(piece, "z", [(0, step), (last, last - step)])
        chunk = jnp.where((slot == step) | (slot == last - step), piece, chunk)
    both = lax.all_gather(chunk, "z", axis=0, tiled=True).reshape(2, rows, local.shape[1])
    lead = jnp.where(owners[0] == 0, 0, 1)
    return lax.dynamic_index_in_dim(both, lead, 0, False), lax.dynamic_index_in_dim(both, 1 - lead, 0, False)


def reduce_rows(part):
    rows, columns = part.shape
    pairs = lax.axis_size("c")
    planes = lax.axis_size("x") * lax.axis_size("y")
    part = lax.all_to_all(part, "c", split_axis=0, concat_axis=0, tiled=True)
    part = part.reshape(pairs, rows // pairs, columns).sum(0)
    tiles = part.reshape(rows // pairs // 8, 8, columns // 128, 128).transpose(0, 2, 1, 3)
    tiles = tiles.reshape(planes, -1, 8, 128)
    tiles = lax.all_to_all(tiles, PLANE, split_axis=0, concat_axis=0, tiled=True)
    total = tiles.sum(0)
    tiles = jnp.broadcast_to(total[None], tiles.shape)
    tiles = lax.all_to_all(tiles, PLANE, split_axis=0, concat_axis=0, tiled=True)
    tiles = tiles.reshape(rows // pairs // 8, columns // 128, 8, 128).transpose(0, 2, 1, 3)
    return lax.all_gather(tiles.reshape(rows // pairs, columns), "c", axis=0, tiled=True)


def per_device(eigvecs, panels, tfactors, owners):
    first, second = gather_panels(panels[0], owners)
    tiles = lax.all_to_all(eigvecs, "z", split_axis=1, concat_axis=0, tiled=True)
    width = first.shape[1]
    total = reduce_rows(jnp.concatenate([tn(first, tiles), tn(second, tiles), tn(second, first)]))
    proj_first, proj_second, cross = total[:width], total[width : 2 * width], total[2 * width :]
    coeff_first = nn(jnp.triu(tfactors[0]), proj_first)
    coeff_second = nn(jnp.triu(tfactors[1]), proj_second - nn(cross, coeff_first))
    return tiles - nn(first, coeff_first) - nn(second, coeff_second)


def solution(mesh):
    split = Mesh(mesh.devices.reshape(4, 8, 2, 8), ("x", "y", "c", "z"))
    rows = ("x", "y", "c")
    placed = (P(rows + ("z",), None), P("z", rows, None), P(), P())
    return jax.shard_map(per_device, mesh=split, in_specs=placed, out_specs=P(rows, "z"), check_vma=False)
```

time: 509 us -> 166 us (0.33)
  waiting for transfers between devices: 430 us -> 72.7 us
  starting transfers between devices: 0.09 us -> 25.1 us
  blocking collectives: 45.1 us -> 35.1 us
    psum x3 -> x0, waiting for transfers between devices: 430 us -> none  [the longest x2 372 us: per_device(): proj = lax.psum(matmul(vectors[index].T, result), 'rows')]
    all_to_all x0 -> x2, waiting for transfers between devices: none -> 47.1 us  [the longest x1 36.3 us: per_device(): lax.all_to_all(eigvecs, 'z', split_axis=1, concat_axis=0, tiled=True)]
    all_to_all x1 -> x2, blocking collectives: 45.1 us -> 28.5 us  [the longest x1 21.4 us: reduce_rows(): lax.all_to_all(tiles, PLANE, split_axis=0, concat_axis=0, tiled=True)]
    all_to_all x0 -> x2, starting transfers between devices: none -> 14.1 us  [the longest x1 7.56 us: reduce_rows(): lax.all_to_all(tiles, PLANE, split_axis=0, concat_axis=0, tiled=True)]
    ppermute x0 -> x3, waiting for transfers between devices: none -> 13.5 us  [gather_panels(): piece = lax.ppermute(piece, 'z', [(0, step), (last, last - step)])]
    all_gather x0 -> x1, waiting for transfers between devices: none -> 12.1 us  [gather_panels(): lax.all_gather(chunk, 'z', axis=0, tiled=True)]
    ppermute x0 -> x3, starting transfers between devices: none -> 11.1 us  [gather_panels(): piece = lax.ppermute(piece, 'z', [(0, step), (last, last - step)])]
    all_gather x0 -> x1, blocking collectives: none -> 6.62 us  [reduce_rows(): lax.all_gather(tiles.reshape(rows // pairs, columns), 'c', axis=0, tiled=...]
  transfers between devices with their start and end apart: 3 -> 6, of which waited for: 3 -> 6; matrix products, arithmetic and copies ran while one was open for 0% -> 1% of each run, Pallas kernels for 0% -> 0%
where the time goes in v1:
time: 166 us; the launch traced here: 165 us
  waiting for transfers between devices  72.7 us (44%)
  blocking collectives  35.1 us (21%)
  starting transfers between devices  25.1 us (15%)
  between operations  13.6 us (8%)
  matrix products  12 us (7%)
  other arithmetic  3.78 us (2%)
  local copies, waits for them, and re-layouts  3.11 us (2%)
    all_to_all x1, waiting for transfers between devices, per_device(): lax.all_to_all(eigvecs, 'z', split_axis=1, concat_axis=0, tiled=True)  36.3 us
    all_to_all x1, blocking collectives, reduce_rows(): lax.all_to_all(tiles, PLANE, split_axis=0, concat_axis=0, tiled=True)  21.4 us
    ppermute x3, waiting for transfers between devices, gather_panels(): piece = lax.ppermute(piece, 'z', [(0, step), (last, last - step)])  13.5 us
    all_gather x1, waiting for transfers between devices, gather_panels(): lax.all_gather(chunk, 'z', axis=0, tiled=True)  12.1 us
    dot_general x8, matrix products, dot(): lax.dot_general(left, right, (dims, ((), ())), precision=HIGHEST, preferr...  12 us
    ppermute x3, starting transfers between devices, gather_panels(): piece = lax.ppermute(piece, 'z', [(0, step), (last, last - step)])  11.1 us
    all_to_all x1, waiting for transfers between devices, reduce_rows(): lax.all_to_all(tiles, PLANE, split_axis=0, concat_axis=0, tiled=True)  10.8 us
    all_to_all x1, starting transfers between devices, reduce_rows(): lax.all_to_all(tiles, PLANE, split_axis=0, concat_axis=0, tiled=True)  7.56 us
  transfers between devices with their start and end apart: 6, of which 6 were waited for; matrix products, arithmetic and copies ran while one was open for 1% of the time, Pallas kernels for 0%

profile of v1, /device:TPU:1, one launch (start us, length us, event | category | flops | bytes accessed | tf_op | source)
XLA Modules:
  0.0 165.4 jit_solution(273788706327266773)
XLA Ops:
  6.5 0.0 all-gather.2.cloned.1.call-start
  6.5 1.2 dynamic-slice_bitcast_fusion
  7.8 8.5 %collective-permute-start = (f32[256,256]{1,0:T(8,128)S(1)}, f32[256,256]{1,0:T(8,128)S(1)}, u32[]{:S(2)}, u32[]{:S(2)}) collective-permute-start(f32[256,256]{1,0:T(8,128)S(1)} %get-tuple-element.7), channel_id=1, source_target_pairs={{0,3},{7,4},{8,11},{15,12},{16,19},{23,20},{24,27},{31,28},{32,35}... | collective-permute-start | bytes 786440 | tf_op jit(solution)/shard_map/ppermute | solution.py:33
  16.3 1.3 collective-permute-start.1
  17.6 1.3 collective-permute-start.2
  18.9 2.3 %collective-permute-done = f32[256,256]{1,0:T(8,128)S(1)} collective-permute-done((f32[256,256]{1,0:T(8,128)S(1)}, f32[256,256]{1,0:T(8,128)S(1)}, u32[]{:S(2)}, u32[]{:S(2)}) %collective-permute-start) | collective-permute-done | bytes 262176 | tf_op jit(solution)/shard_map/ppermute | solution.py:33
  21.2 5.6 %collective-permute-done.1 = f32[256,256]{1,0:T(8,128)S(1)} collective-permute-done((f32[256,256]{1,0:T(8,128)S(1)}, f32[256,256]{1,0:T(8,128)S(1)}, u32[]{:S(2)}, u32[]{:S(2)}) %collective-permute-start.1) | collective-permute-done | bytes 262176 | tf_op jit(solution)/shard_map/ppermute | solution.py:33
  26.8 5.6 %collective-permute-done.2 = f32[256,256]{1,0:T(8,128)S(1)} collective-permute-done((f32[256,256]{1,0:T(8,128)S(1)}, f32[256,256]{1,0:T(8,128)S(1)}, u32[]{:S(2)}, u32[]{:S(2)}) %collective-permute-start.2) | collective-permute-done | bytes 262176 | tf_op jit(solution)/shard_map/ppermute | solution.py:33
  32.4 1.7 %fusion.20 = f32[256,256]{1,0:T(8,128)} fusion(f32[256,256]{1,0:T(8,128)S(1)} %collective-permute-done, f32[256,256]{1,0:T(8,128)S(1)} %collective-permute-done.1, f32[256,256]{1,0:T(8,128)S(1)} %collective-permute-done.2, f32[1,1024,256]{2,1,0:T(8,128)} %param.5, s32[]{:T(128)S(6)} %select_n.61, pred[]{:T(512)S(6)} %or.11, pred[]{:T(512)S(6)} %or.10, pred[]{:T(512)S(6)} %or.9), kind=kLoop, calls=%fused_computation.28 | loop fusion | flops 196608 | bytes 1310727 | tf_op jit(solution)/shard_map/jit(_where)/select_n | solution.py:34
  34.1 0.0 all-gather.2.cloned.1.call-update
  34.2 0.0 copy-start.3
  34.2 1.1 copy.9
  35.3 6.5 %all-to-all-start = ((f32[128,8,256]{2,0,1:T(8,128)}), f32[128,8,256]{2,0,1:T(8,128)S(1)}, u32[]{:S(2)}, u32[]{:S(2)}) async-start(f32[128,8,256]{2,0,1:T(8,128)} %bitcast.57), calls=%async_computation | async-start | bytes 2097152 | tf_op jit(solution)/shard_map/all_to_all | solution.py:58
  41.8 36.3 %all-to-all-done = f32[128,8,256]{2,0,1:T(8,128)S(1)} async-done(((f32[128,8,256]{2,0,1:T(8,128)}), f32[128,8,256]{2,0,1:T(8,128)S(1)}, u32[]{:S(2)}, u32[]{:S(2)}) %all-to-all-start) | async-done | bytes 1048608 | tf_op jit(solution)/shard_map/all_to_all | solution.py:58
  78.1 12.1 %all-gather.2.cloned.1.call-done = f32[2048,256]{1,0:T(8,128)} async-done(((f32[256,256]{1,0:T(8,128)}), f32[2048,256]{1,0:T(8,128)}) %all-gather.2.cloned.1.call-update) | async-done | bytes 2097168 | tf_op jit(solution)/shard_map/all_gather | solution.py:35
  90.2 3.2 %fusion.7 = f32[256,256]{1,0:T(8,128)S(1)} fusion(f32[1024,256]{1,0:T(8,128)S(1)} %bitcast.64, f32[2,1024,256]{2,1,0:T(8,128)} %bitcast.59, s32[]{:T(128)} %bitcast.7), kind=kOutput, calls=%fused_computation.11 | convolution fusion | flops 805306368 | bytes 2359808 | tf_op jit(solution)/shard_map/dot_general | solution.py:11
  93.4 1.8 %fusion.3 = f32[256,256]{1,0:T(8,128)S(1)} fusion(f32[1024,256]{1,0:T(8,128)S(1)} %bitcast.65, f32[2,1024,256]{2,1,0:T(8,128)S(1)} %bitcast.60, s32[]{:T(128)S(6)} %select_n.68), kind=kOutput, calls=%fused_computation.7 | convolution fusion | flops 805306368 | bytes 2359300 | tf_op jit(solution)/shard_map/dot_general | solution.py:11
  95.2 1.8 %fusion.1 = f32[256,256]{1,0:T(8,128)S(1)} fusion(f32[2,1024,256]{2,1,0:T(8,128)S(1)} %bitcast.61, s32[]{:T(128)S(6)} %select_n.68, s32[]{:T(128)} %bitcast.7), kind=kOutput, calls=%fused_computation.5 | convolution fusion | flops 805306368 | bytes 2359304 | tf_op jit(solution)/shard_map/dot_general | solution.py:11
  97.1 0.1 pad_maximum_fusion
  97.1 7.0 %all_to_all.38 = f32[2,384,256]{2,1,0:T(8,128)} all-to-all(f32[2,384,256]{2,1,0:T(8,128)S(1)} %bitcast.67), channel_id=1, replica_groups=mesh['x'=4,'y'=8,'c'=2,'z'=8] {'c'}, dimensions={0} | all-to-all | bytes 1572864 | tf_op jit(solution)/shard_map/all_to_all | solution.py:44
  104.2 2.0 %reduce_sum.18 = f32[384,256]{1,0:T(8,128)} reduce(f32[2,384,256]{2,1,0:T(8,128)} %all_to_all.38, f32[]{:T(128)} %constant.56.clone.1), dimensions={0}, to_apply=%region_0.1 | reduce | flops 98304 | bytes 1179652 | tf_op jit(solution)/shard_map/reduce_sum | solution.py:45
  106.1 21.4 %all_to_all.39 = f32[32,3,8,128]{3,2,1,0:T(8,128)S(1)} all-to-all(f32[32,3,8,128]{3,2,1,0:T(8,128)} %bitcast.69), channel_id=1, replica_groups=mesh['x'=4,'y'=8,'c'=2,'z'=8] {'x','y'}, dimensions={0} | all-to-all | bytes 786432 | tf_op jit(solution)/shard_map/all_to_all | solution.py:48
  127.6 0.8 broadcast_in_dim.12
  128.4 7.6 %all-to-all-start.3 = ((f32[32,3,8,128]{3,2,1,0:T(8,128)}), f32[32,3,8,128]{3,2,1,0:T(8,128)S(1)}, u32[]{:S(2)}, u32[]{:S(2)}) async-start(f32[32,3,8,128]{3,2,1,0:T(8,128)} %broadcast_in_dim.12), calls=%async_computation.3 | async-start | bytes 786432 | tf_op jit(solution)/shard_map/all_to_all | solution.py:51
  136.0 10.8 %all-to-all-done.3 = f32[32,3,8,128]{3,2,1,0:T(8,128)S(1)} async-done(((f32[32,3,8,128]{3,2,1,0:T(8,128)}), f32[32,3,8,128]{3,2,1,0:T(8,128)S(1)}, u32[]{:S(2)}, u32[]{:S(2)}) %all-to-all-start.3) | async-done | bytes 393248 | tf_op jit(solution)/shard_map/all_to_all | solution.py:51
  146.8 6.6 %all_gather.7 = f32[768,256]{1,0:T(8,128)S(1)} all-gather(f32[384,256]{1,0:T(8,128)S(1)} %bitcast.68), channel_id=1, replica_groups=mesh['x'=4,'y'=8,'c'=2,'z'=8] {'c'}, dimensions={0}, use_global_device_ids=true | all-gather | bytes 1179648 | tf_op jit(solution)/shard_map/all_gather | solution.py:53
  153.4 1.4 fusion.16
  154.8 0.0 copy-start.2
  154.8 0.4 convolution_subtract_fusion.2
  155.2 1.0 convolution_subtract_fusion.1
  156.2 0.4 fusion.18
  156.6 2.0 %convolution_subtract_fusion = f32[1024,256]{1,0:T(8,128)} fusion(f32[1024,256]{1,0:T(8,128)S(1)} %convolution_subtract_fusion.1, f32[256,256]{1,0:T(8,128)S(1)} %fusion.18, f32[2,1024,256]{2,1,0:T(8,128)S(1)} %bitcast.63, s32[]{:T(128)S(6)} %select_n.68), kind=kOutput, calls=%fused_computation | convolution fusion | flops 805568512 | bytes 3407876 | tf_op jit(solution)/shard_map/dot_general | solution.py:11
  (8 shorter events, 0.1 us)
Async XLA Ops:
  6.5 27.6 %copy-start.1 = (f32[128,2048]{1,0:T(8,128)S(1)}, f32[128,2048]{1,0:T(8,128)}, u32[]{:S(2)}) copy-start(f32[128,2048]{1,0:T(8,128)} %param.4) | copy-start | bytes 3145732
  6.5 83.6 %all-gather.2.cloned.1.call-start = ((), (), s32[]{:S(2)}) async-start(), calls=%async_computation.4 | async-start | bytes 2359296 | tf_op jit(solution)/shard_map/all_gather | solution.py:35
  7.8 13.4 %collective-permute-start = (f32[256,256]{1,0:T(8,128)S(1)}, f32[256,256]{1,0:T(8,128)S(1)}, u32[]{:S(2)}, u32[]{:S(2)}) collective-permute-start(f32[256,256]{1,0:T(8,128)S(1)} %get-tuple-element.7), channel_id=1, source_target_pairs={{0,3},{7,4},{8,11},{15,12},{16,19},{23,20},{24,27},{31,28},{32,35}... | collective-permute-start | bytes 786440 | tf_op jit(solution)/shard_map/ppermute | solution.py:33
  16.3 10.6 %collective-permute-start.1 = (f32[256,256]{1,0:T(8,128)S(1)}, f32[256,256]{1,0:T(8,128)S(1)}, u32[]{:S(2)}, u32[]{:S(2)}) collective-permute-start(f32[256,256]{1,0:T(8,128)S(1)} %get-tuple-element.6), channel_id=1, source_target_pairs={{0,2},{7,5},{8,10},{15,13},{16,18},{23,21},{24,26},{31,29},{32,34}... | collective-permute-start | bytes 786440 | tf_op jit(solution)/shard_map/ppermute | solution.py:33
  17.6 14.9 %collective-permute-start.2 = (f32[256,256]{1,0:T(8,128)S(1)}, f32[256,256]{1,0:T(8,128)S(1)}, u32[]{:S(2)}, u32[]{:S(2)}) collective-permute-start(f32[256,256]{1,0:T(8,128)S(1)} %get-tuple-element.5), channel_id=1, source_target_pairs={{0,1},{7,6},{8,9},{15,14},{16,17},{23,22},{24,25},{31,30},{32,33},... | collective-permute-start | bytes 786440 | tf_op jit(solution)/shard_map/ppermute | solution.py:33
  34.2 7.6 %copy-start.3 = (s32[2]{0:T(128)S(1)}, s32[2]{0:T(128)}, u32[]{:S(2)}) copy-start(s32[2]{0:T(128)} %param.7) | copy-start | bytes 28
  35.3 42.8 %all-to-all-start = ((f32[128,8,256]{2,0,1:T(8,128)}), f32[128,8,256]{2,0,1:T(8,128)S(1)}, u32[]{:S(2)}, u32[]{:S(2)}) async-start(f32[128,8,256]{2,0,1:T(8,128)} %bitcast.57), calls=%async_computation | async-start | bytes 2097152 | tf_op jit(solution)/shard_map/all_to_all | solution.py:58
  90.2 3.2 %copy-start = (f32[2048,256]{1,0:T(8,128)S(1)}, f32[2048,256]{1,0:T(8,128)}, u32[]{:S(2)}) copy-start(f32[2048,256]{1,0:T(8,128)} %all-gather.2.cloned.1.call-done) | copy-start | bytes 6291460
  128.4 18.4 %all-to-all-start.3 = ((f32[32,3,8,128]{3,2,1,0:T(8,128)}), f32[32,3,8,128]{3,2,1,0:T(8,128)S(1)}, u32[]{:S(2)}, u32[]{:S(2)}) async-start(f32[32,3,8,128]{3,2,1,0:T(8,128)} %broadcast_in_dim.12), calls=%async_computation.3 | async-start | bytes 786432 | tf_op jit(solution)/shard_map/all_to_all | solution.py:51
  154.8 1.4 copy-start.2
Sparse Core Ops, SparseCore 0:
  34.3 55.8 all-gather.1

commit v2 on v1

v2 whole, which is shorter than its diff:
```python
import jax
import jax.numpy as jnp
from jax import lax
from jax.sharding import Mesh, PartitionSpec as P

PLANE = ("x", "y")


def dot(left, right, dims):
    return lax.dot_general(
        left, right, (dims, ((), ())), precision=lax.Precision.HIGH, preferred_element_type=jnp.float32
    )


def tn(left, right):
    return dot(left, right, ((0,), (0,)))


def nn(left, right):
    return dot(left, right, ((1,), (0,)))


def shift(value, by):
    count = lax.axis_size("z")
    return lax.ppermute(value, "z", [(slot, (slot + by) % count) for slot in range(count)])


def owner_quarters(local):
    quarter = local.shape[0] // 4
    last = lax.axis_index("z") == lax.axis_size("z") - 1
    starts = [jnp.where(last, (3 - step) * quarter, step * quarter) for step in range(4)]
    return [lax.dynamic_slice_in_dim(local, start, quarter) for start in starts]


def scatter_quarters(pieces):
    slot = lax.axis_index("z")
    last = lax.axis_size("z") - 1
    chunk = pieces[0]
    for step in range(1, 4):
        piece = lax.ppermute(pieces[step], "z", [(0, step), (last, last - step)])
        chunk = jnp.where((slot == step) | (slot == last - step), piece, chunk)
    return chunk


def gather_panels(chunk):
    rows, width = chunk.shape
    before2, after2 = shift(chunk, 2), shift(chunk, -2)
    before1, after1 = shift(chunk, 1), shift(chunk, -1)
    after3, before3 = shift(after2, -1), shift(before2, 1)
    across = jnp.concatenate([shift(after2[: rows // 2], -2), shift(before2[rows // 2 :], 2)])
    before, after = [chunk, before1, before2, before3], [chunk, after1, after2, after3]
    slot = lax.axis_index("z")
    both = jnp.zeros((8, rows, width), chunk.dtype)
    for by, piece in enumerate(before):
        both = lax.dynamic_update_index_in_dim(both, piece, (slot - by) % 8, 0)
    for by, piece in enumerate(after[1:]):
        both = lax.dynamic_update_index_in_dim(both, piece, (slot + by + 1) % 8, 0)
    both = lax.dynamic_update_index_in_dim(both, across, (slot + 4) % 8, 0)
    return both.reshape(2, 4 * rows, width)


def products(first, second, tiles, half):
    width = tiles.shape[1] // 2
    tiles, other = (lax.dynamic_slice_in_dim(value, half * width, width, 1) for value in (tiles, first))
    return jnp.concatenate([tn(first, tiles), tn(second, tiles), tn(second, other)])


def reduce_rows(first, second, tiles):
    core = lax.axis_index("c")
    other = products(first, second, tiles, 1 - core)
    other = lax.ppermute(other, "c", [(0, 1), (1, 0)])
    part = products(first, second, tiles, core) + other
    rows, columns = part.shape
    planes = lax.axis_size("x") * lax.axis_size("y")
    pieces = part.reshape(planes, rows // planes, columns)
    pieces = lax.all_to_all(pieces, PLANE, split_axis=0, concat_axis=0, tiled=True)
    pieces = jnp.broadcast_to(pieces.sum(0)[None], pieces.shape)
    pieces = lax.all_to_all(pieces, PLANE, split_axis=0, concat_axis=0, tiled=True)
    return lax.all_gather(pieces.reshape(rows, columns), "c", axis=1, tiled=True)


def per_device(eigvecs, panels, tfactors, owners):
    pieces = owner_quarters(panels[0])
    pieces, eigvecs = lax.optimization_barrier((pieces, eigvecs))
    chunk = scatter_quarters(pieces)
    factors = jnp.triu(tfactors)
    count = lax.axis_size("z")
    tiles = eigvecs.reshape(eigvecs.shape[0], count, -1).swapaxes(0, 1)
    chunk, tiles, factors = lax.optimization_barrier((chunk, tiles, factors))
    tiles = lax.all_to_all(tiles, "z", split_axis=0, concat_axis=0, tiled=True)
    tiles = tiles.reshape(-1, tiles.shape[2])
    both = gather_panels(chunk)
    lead = jnp.where(owners[0] == 0, 0, 1)
    first = lax.dynamic_index_in_dim(both, lead, 0, False)
    second = lax.dynamic_index_in_dim(both, 1 - lead, 0, False)
    width = first.shape[1]
    total = reduce_rows(first, second, tiles)
    proj_first, proj_second, cross = total[:width], total[width : 2 * width], total[2 * width :]
    coeff_first = nn(factors[0], proj_first)
    coeff_second = nn(factors[1], proj_second - nn(cross, coeff_first))
    return tiles - nn(first, coeff_first) - nn(second, coeff_second)


def solution(mesh):
    split = Mesh(mesh.devices.reshape(4, 8, 2, 8), ("x", "y", "c", "z"))
    rows = ("x", "y", "c")
    placed = (P(rows + ("z",), None), P("z", rows, None), P(), P())
    return jax.shard_map(per_device, mesh=split, in_specs=placed, out_specs=P(rows, "z"), check_vma=False)
```

time: 166 us -> 147 us (0.89)
  waiting for transfers between devices: 72.7 us -> 31 us
  starting transfers between devices: 25.1 us -> 48.9 us
  between operations: 13.6 us -> 0.56 us
  blocking collectives: 35.1 us -> 46.5 us
  local copies, waits for them, and re-layouts: 3.11 us -> 8.46 us
  matrix products: 12 us -> 9.29 us
  other arithmetic: 3.78 us -> 1.9 us
    all_to_all x2 -> x1, waiting for transfers between devices: 47.1 us -> 0.01 us  [per_device(): tiles = lax.all_to_all(tiles, 'z', split_axis=0, concat_axis=0, tiled=True)]
    ppermute x3 -> x12, starting transfers between devices: 11.1 us -> 45.4 us  [the longest x8 30.5 us: shift(): lax.ppermute(value, 'z', [(slot, (slot + by) % count) for slot in range(c...]
    ppermute x3 -> x12, waiting for transfers between devices: 13.5 us -> 31 us  [the longest x8 20.9 us: shift(): lax.ppermute(value, 'z', [(slot, (slot + by) % count) for slot in range(c...]
    all_gather x1 -> x0, waiting for transfers between devices: 12.1 us -> none  [gather_panels(): lax.all_gather(chunk, 'z', axis=0, tiled=True)]
    all_to_all x2, blocking collectives: 28.5 us -> 40.3 us  [reduce_rows(): lax.all_to_all(pieces, PLANE, split_axis=0, concat_axis=0, tiled=True)]
    all_to_all x2 -> x1, starting transfers between devices: 14.1 us -> 3.57 us  [per_device(): tiles = lax.all_to_all(tiles, 'z', split_axis=0, concat_axis=0, tiled=True)]
    dynamic_update_slice x0 -> x7, local copies, waits for them, and re-layouts: none -> 3.97 us  [the longest x4 1.99 us: gather_panels(): both = lax.dynamic_update_index_in_dim(both, piece, (slot - by) % 8, 0)]
    dot_general x8 -> x11, matrix products: 12 us -> 9.29 us  [dot(): lax.dot_general(left, right, (dims, ((), ())), precision=lax.Precision.HI...]
  transfers between devices with their start and end apart: 6 -> 13, of which waited for: 6 -> 3; matrix products, arithmetic and copies ran while one was open for 1% -> 8% of each run, Pallas kernels for 0% -> 0%
where the time goes in v2:
time: 147 us
  starting transfers between devices  48.9 us (33%)
  blocking collectives  46.5 us (32%)
  waiting for transfers between devices  31 us (21%)
  matrix products  9.29 us (6%)
  local copies, waits for them, and re-layouts  8.46 us (6%)
  other arithmetic  1.9 us (1%)
    all_to_all x2, blocking collectives, reduce_rows(): lax.all_to_all(pieces, PLANE, split_axis=0, concat_axis=0, tiled=True)  40.3 us
    ppermute x8, starting transfers between devices, shift(): lax.ppermute(value, 'z', [(slot, (slot + by) % count) for slot in range(c...  30.5 us
    ppermute x8, waiting for transfers between devices, shift(): lax.ppermute(value, 'z', [(slot, (slot + by) % count) for slot in range(c...  20.9 us
    ppermute x3, starting transfers between devices, scatter_quarters(): piece = lax.ppermute(pieces[step], 'z', [(0, step), (last, last - step)])  12.5 us
    ppermute x3, waiting for transfers between devices, scatter_quarters(): piece = lax.ppermute(pieces[step], 'z', [(0, step), (last, last - step)])  10.1 us
    dot_general x11, matrix products, dot(): lax.dot_general(left, right, (dims, ((), ())), precision=lax.Precision.HI...  9.29 us
    all_gather x1, blocking collectives, reduce_rows(): lax.all_gather(pieces.reshape(rows, columns), 'c', axis=1, tiled=True)  6.22 us
    all_to_all x1, starting transfers between devices, per_device(): tiles = lax.all_to_all(tiles, 'z', split_axis=0, concat_axis=0, tiled=True)  3.57 us
  transfers between devices with their start and end apart: 13, of which 3 were waited for; matrix products, arithmetic and copies ran while one was open for 8% of the time, Pallas kernels for 0%

profile of v2, /device:TPU:1, one launch (start us, length us, event | category | flops | bytes accessed | tf_op | source)
XLA Modules:
  0.0 146.7 jit_solution(18208789601227877676)
XLA Ops:
  0.0 1.4 dynamic-slice_bitcast_fusion
  1.4 8.5 %collective-permute-start = (f32[256,256]{1,0:T(8,128)S(1)}, f32[256,256]{1,0:T(8,128)S(1)}, u32[]{:S(2)}, u32[]{:S(2)}) collective-permute-start(f32[256,256]{1,0:T(8,128)S(1)} %get-tuple-element.13), channel_id=1, source_target_pairs={{0,3},{7,4},{8,11},{15,12},{16,19},{23,20},{24,27},{31,28},{32,35}... | collective-permute-start | bytes 786440 | tf_op jit(solution)/shard_map/ppermute | solution.py:40
  9.9 2.0 %collective-permute-start.1 = (f32[256,256]{1,0:T(8,128)S(1)}, f32[256,256]{1,0:T(8,128)}, u32[]{:S(2)}, u32[]{:S(2)}) collective-permute-start(f32[256,256]{1,0:T(8,128)S(1)} %get-tuple-element.14), channel_id=1, source_target_pairs={{0,2},{7,5},{8,10},{15,13},{16,18},{23,21},{24,26},{31,29},{32,34}... | collective-permute-start | bytes 786440 | tf_op jit(solution)/shard_map/ppermute | solution.py:40
  11.9 2.0 %collective-permute-start.2 = (f32[256,256]{1,0:T(8,128)S(1)}, f32[256,256]{1,0:T(8,128)}, u32[]{:S(2)}, u32[]{:S(2)}) collective-permute-start(f32[256,256]{1,0:T(8,128)S(1)} %get-tuple-element.15), channel_id=1, source_target_pairs={{0,1},{7,6},{8,9},{15,14},{16,17},{23,22},{24,25},{31,30},{32,33},... | collective-permute-start | bytes 786440 | tf_op jit(solution)/shard_map/ppermute | solution.py:40
  14.0 1.1 copy.8
  15.9 4.5 %collective-permute-done.1 = f32[256,256]{1,0:T(8,128)} collective-permute-done((f32[256,256]{1,0:T(8,128)S(1)}, f32[256,256]{1,0:T(8,128)}, u32[]{:S(2)}, u32[]{:S(2)}) %collective-permute-start.1) | collective-permute-done | bytes 262176 | tf_op jit(solution)/shard_map/ppermute | solution.py:40
  20.4 5.6 %collective-permute-done.2 = f32[256,256]{1,0:T(8,128)} collective-permute-done((f32[256,256]{1,0:T(8,128)S(1)}, f32[256,256]{1,0:T(8,128)}, u32[]{:S(2)}, u32[]{:S(2)}) %collective-permute-start.2) | collective-permute-done | bytes 262176 | tf_op jit(solution)/shard_map/ppermute | solution.py:40
  26.1 1.9 %collective-permute-start.4 = (f32[256,256]{1,0:T(8,128)S(1)}, f32[256,256]{1,0:T(8,128)}, u32[]{:S(2)}, u32[]{:S(2)}) collective-permute-start(f32[256,256]{1,0:T(8,128)S(1)} %select_select_fusion), channel_id=1, source_target_pairs={{0,2},{1,3},{2,4},{3,5},{4,6},{5,7},{6,0},{7,1},{8,10},{9,11},{10,... | collective-permute-start | bytes 786440 | tf_op jit(solution)/shard_map/ppermute | solution.py:25
  28.0 8.2 %collective-permute-start.7 = (f32[256,256]{1,0:T(8,128)S(1)}, f32[256,256]{1,0:T(8,128)}, u32[]{:S(2)}, u32[]{:S(2)}) collective-permute-start(f32[256,256]{1,0:T(8,128)S(1)} %select_select_fusion), channel_id=1, source_target_pairs={{0,6},{1,7},{2,0},{3,1},{4,2},{5,3},{6,4},{7,5},{8,14},{9,15},{10,... | collective-permute-start | bytes 786440 | tf_op jit(solution)/shard_map/ppermute | solution.py:25
  36.2 2.5 %collective-permute-start.3 = (f32[256,256]{1,0:T(8,128)S(1)}, f32[256,256]{1,0:T(8,128)}, u32[]{:S(2)}, u32[]{:S(2)}) collective-permute-start(f32[256,256]{1,0:T(8,128)S(1)} %select_select_fusion), channel_id=1, source_target_pairs={{0,1},{1,2},{2,3},{3,4},{4,5},{5,6},{6,7},{7,0},{8,9},{9,10},{10,1... | collective-permute-start | bytes 786440 | tf_op jit(solution)/shard_map/ppermute | solution.py:25
  38.9 4.0 %collective-permute-start.6 = (f32[256,256]{1,0:T(8,128)S(1)}, f32[256,256]{1,0:T(8,128)}, u32[]{:S(2)}, u32[]{:S(2)}) collective-permute-start(f32[256,256]{1,0:T(8,128)S(1)} %select_select_fusion), channel_id=1, source_target_pairs={{0,7},{1,0},{2,1},{3,2},{4,3},{5,4},{6,5},{7,6},{8,15},{9,8},{10,9... | collective-permute-start | bytes 786440 | tf_op jit(solution)/shard_map/ppermute | solution.py:25
  42.9 3.6 %all-to-all-start = ((f32[8,128,256]{2,1,0:T(8,128)}), f32[8,128,256]{2,1,0:T(8,128)S(1)}, u32[]{:S(2)}, u32[]{:S(2)}) async-start(f32[8,128,256]{2,1,0:T(8,128)} %bitcast.71), calls=%async_computation | async-start | bytes 2097152 | tf_op jit(solution)/shard_map/all_to_all | solution.py:90
  47.6 4.2 %collective-permute-start.10 = (f32[128,256]{1,0:T(8,128)S(1)}, f32[128,256]{1,0:T(8,128)S(1)}, u32[]{:S(2)}, u32[]{:S(2)}) collective-permute-start(f32[128,256]{1,0:T(8,128)S(1)} %slice.33), channel_id=1, source_target_pairs={{0,2},{1,3},{2,4},{3,5},{4,6},{5,7},{6,0},{7,1},{8,10},{9,11},{10,... | collective-permute-start | bytes 393224 | tf_op jit(solution)/shard_map/ppermute | solution.py:25
  52.8 3.2 %collective-permute-start.9 = (f32[128,256]{1,0:T(8,128)S(1)}, f32[128,256]{1,0:T(8,128)S(1)}, u32[]{:S(2)}, u32[]{:S(2)}) collective-permute-start(f32[128,256]{1,0:T(8,128)S(1)} %slice.32), channel_id=1, source_target_pairs={{0,6},{1,7},{2,0},{3,1},{4,2},{5,3},{6,4},{7,5},{8,14},{9,15},{10,... | collective-permute-start | bytes 393224 | tf_op jit(solution)/shard_map/ppermute | solution.py:25
  56.0 3.3 %collective-permute-start.5 = (f32[256,256]{1,0:T(8,128)}, f32[256,256]{1,0:T(8,128)S(1)}, u32[]{:S(2)}, u32[]{:S(2)}) collective-permute-start(f32[256,256]{1,0:T(8,128)} %collective-permute-done.4), channel_id=1, source_target_pairs={{0,1},{1,2},{2,3},{3,4},{4,5},{5,6},{6,7},{7,0},{8,9},{9,10},{10,1... | collective-permute-start | bytes 786440 | tf_op jit(solution)/shard_map/ppermute | solution.py:25
  59.3 3.2 %collective-permute-start.8 = (f32[256,256]{1,0:T(8,128)}, f32[256,256]{1,0:T(8,128)S(1)}, u32[]{:S(2)}, u32[]{:S(2)}) collective-permute-start(f32[256,256]{1,0:T(8,128)} %collective-permute-done.7), channel_id=1, source_target_pairs={{0,7},{1,0},{2,1},{3,2},{4,3},{5,4},{6,5},{7,6},{8,15},{9,8},{10,9... | collective-permute-start | bytes 786440 | tf_op jit(solution)/shard_map/ppermute | solution.py:25
  62.5 1.0 bitcast_dynamic-update-slice_fusion.5
  63.5 1.0 bitcast_dynamic-update-slice_fusion.4
  64.5 20.9 %collective-permute-done.5 = f32[256,256]{1,0:T(8,128)S(1)} collective-permute-done((f32[256,256]{1,0:T(8,128)}, f32[256,256]{1,0:T(8,128)S(1)}, u32[]{:S(2)}, u32[]{:S(2)}) %collective-permute-start.5) | collective-permute-done | bytes 262176 | tf_op jit(solution)/shard_map/ppermute | solution.py:25
  85.4 1.0 bitcast_dynamic-update-slice_fusion.2
  86.4 1.0 bitcast_dynamic-update-slice_fusion.1
  87.4 1.2 fusion.1
  88.6 1.0 fusion.10
  89.6 1.0 fusion.3
  91.4 2.4 %collective-permute-start.11 = (f32[768,128]{1,0:T(8,128)}, f32[768,128]{1,0:T(8,128)S(1)}, u32[]{:S(2)}, u32[]{:S(2)}) collective-permute-start(f32[768,128]{1,0:T(8,128)} %pad_maximum_fusion), channel_id=1, source_target_pairs={{0,8},{8,0},{1,9},{9,1},{2,10},{10,2},{3,11},{11,3},{4,12},{12,4},... | collective-permute-start | bytes 1179656 | tf_op jit(solution)/shard_map/ppermute | solution.py:71
  93.8 1.2 fusion.5
  95.0 1.0 fusion.12
  96.0 1.0 fusion.7
  97.1 21.7 %all_to_all.15 = f32[32,24,128]{2,1,0:T(8,128)S(1)} all-to-all(f32[32,24,128]{2,1,0:T(8,128)S(1)} %bitcast.86), channel_id=1, replica_groups=mesh['x'=4,'y'=8,'c'=2,'z'=8] {'x','y'}, dimensions={0} | all-to-all | bytes 786432 | tf_op jit(solution)/shard_map/all_to_all | solution.py:76
  118.9 18.6 %all_to_all.16 = f32[32,24,128]{2,1,0:T(8,128)S(1)} all-to-all(f32[32,24,128]{2,1,0:T(8,128)S(1)} %broadcast_in_dim.53), channel_id=1, replica_groups=mesh['x'=4,'y'=8,'c'=2,'z'=8] {'x','y'}, dimensions={0} | all-to-all | bytes 786432 | tf_op jit(solution)/shard_map/all_to_all | solution.py:78
  137.5 6.2 %all_gather.3 = f32[768,256]{1,0:T(8,128)S(1)} all-gather(f32[768,128]{1,0:T(8,128)S(1)} %bitcast.87), channel_id=1, replica_groups=mesh['x'=4,'y'=8,'c'=2,'z'=8] {'c'}, dimensions={1}, use_global_device_ids=true | all-gather | bytes 1179648 | tf_op jit(solution)/shard_map/all_gather | solution.py:79
  145.1 1.6 %convolution_subtract_fusion = f32[1024,256]{1,0:T(8,128)} fusion(f32[1024,256]{1,0:T(8,128)S(1)} %convolution_subtract_fusion.1, f32[256,256]{1,0:T(8,128)S(1)} %fusion.34, f32[2,1024,256]{2,1,0:T(8,128)S(1)} %bitcast.80, s32[]{:T(128)S(6)} %select_n.156), kind=kOutput, calls=%fused_computation | convolution fusion | flops 402915328 | bytes 3407876 | tf_op jit(solution)/shard_map/dot_general | solution.py:10
  (37 shorter events, 5.4 us)
Async XLA Ops:
  0.0 14.0 %copy-start.1 = (f32[128,2048]{1,0:T(8,128)S(1)}, f32[128,2048]{1,0:T(8,128)}, u32[]{:S(2)}) copy-start(f32[128,2048]{1,0:T(8,128)} %param.4) | copy-start | bytes 3145732
  0.0 15.1 %copy-start.2 = (f32[2,256,256]{2,1,0:T(8,128)S(1)}, f32[2,256,256]{2,1,0:T(8,128)}, u32[]{:S(2)}) copy-start(f32[2,256,256]{2,1,0:T(8,128)} %param.6) | copy-start | bytes 1572868
  1.4 14.5 %collective-permute-start = (f32[256,256]{1,0:T(8,128)S(1)}, f32[256,256]{1,0:T(8,128)S(1)}, u32[]{:S(2)}, u32[]{:S(2)}) collective-permute-start(f32[256,256]{1,0:T(8,128)S(1)} %get-tuple-element.13), channel_id=1, source_target_pairs={{0,3},{7,4},{8,11},{15,12},{16,19},{23,20},{24,27},{31,28},{32,35}... | collective-permute-start | bytes 786440 | tf_op jit(solution)/shard_map/ppermute | solution.py:40
  9.9 10.6 %collective-permute-start.1 = (f32[256,256]{1,0:T(8,128)S(1)}, f32[256,256]{1,0:T(8,128)}, u32[]{:S(2)}, u32[]{:S(2)}) collective-permute-start(f32[256,256]{1,0:T(8,128)S(1)} %get-tuple-element.14), channel_id=1, source_target_pairs={{0,2},{7,5},{8,10},{15,13},{16,18},{23,21},{24,26},{31,29},{32,34}... | collective-permute-start | bytes 786440 | tf_op jit(solution)/shard_map/ppermute | solution.py:40
  11.9 14.2 %collective-permute-start.2 = (f32[256,256]{1,0:T(8,128)S(1)}, f32[256,256]{1,0:T(8,128)}, u32[]{:S(2)}, u32[]{:S(2)}) collective-permute-start(f32[256,256]{1,0:T(8,128)S(1)} %get-tuple-element.15), channel_id=1, source_target_pairs={{0,1},{7,6},{8,9},{15,14},{16,17},{23,22},{24,25},{31,30},{32,33},... | collective-permute-start | bytes 786440 | tf_op jit(solution)/shard_map/ppermute | solution.py:40
  14.0 24.8 %copy-start.3 = (s32[2]{0:T(128)S(1)}, s32[2]{0:T(128)}, u32[]{:S(2)}) copy-start(s32[2]{0:T(128)} %param.7) | copy-start | bytes 28
  26.1 20.6 %collective-permute-start.4 = (f32[256,256]{1,0:T(8,128)S(1)}, f32[256,256]{1,0:T(8,128)}, u32[]{:S(2)}, u32[]{:S(2)}) collective-permute-start(f32[256,256]{1,0:T(8,128)S(1)} %select_select_fusion), channel_id=1, source_target_pairs={{0,2},{1,3},{2,4},{3,5},{4,6},{5,7},{6,0},{7,1},{8,10},{9,11},{10,... | collective-permute-start | bytes 786440 | tf_op jit(solution)/shard_map/ppermute | solution.py:25
  28.0 23.8 %collective-permute-start.7 = (f32[256,256]{1,0:T(8,128)S(1)}, f32[256,256]{1,0:T(8,128)}, u32[]{:S(2)}, u32[]{:S(2)}) collective-permute-start(f32[256,256]{1,0:T(8,128)S(1)} %select_select_fusion), channel_id=1, source_target_pairs={{0,6},{1,7},{2,0},{3,1},{4,2},{5,3},{6,4},{7,5},{8,14},{9,15},{10,... | collective-permute-start | bytes 786440 | tf_op jit(solution)/shard_map/ppermute | solution.py:25
  36.2 23.0 %collective-permute-start.3 = (f32[256,256]{1,0:T(8,128)S(1)}, f32[256,256]{1,0:T(8,128)}, u32[]{:S(2)}, u32[]{:S(2)}) collective-permute-start(f32[256,256]{1,0:T(8,128)S(1)} %select_select_fusion), channel_id=1, source_target_pairs={{0,1},{1,2},{2,3},{3,4},{4,5},{5,6},{6,7},{7,0},{8,9},{9,10},{10,1... | collective-permute-start | bytes 786440 | tf_op jit(solution)/shard_map/ppermute | solution.py:25
  38.9 46.5 %collective-permute-start.6 = (f32[256,256]{1,0:T(8,128)S(1)}, f32[256,256]{1,0:T(8,128)}, u32[]{:S(2)}, u32[]{:S(2)}) collective-permute-start(f32[256,256]{1,0:T(8,128)S(1)} %select_select_fusion), channel_id=1, source_target_pairs={{0,7},{1,0},{2,1},{3,2},{4,3},{5,4},{6,5},{7,6},{8,15},{9,8},{10,9... | collective-permute-start | bytes 786440 | tf_op jit(solution)/shard_map/ppermute | solution.py:25
  42.9 45.7 %all-to-all-start = ((f32[8,128,256]{2,1,0:T(8,128)}), f32[8,128,256]{2,1,0:T(8,128)S(1)}, u32[]{:S(2)}, u32[]{:S(2)}) async-start(f32[8,128,256]{2,1,0:T(8,128)} %bitcast.71), calls=%async_computation | async-start | bytes 2097152 | tf_op jit(solution)/shard_map/all_to_all | solution.py:90
  47.6 39.7 %collective-permute-start.10 = (f32[128,256]{1,0:T(8,128)S(1)}, f32[128,256]{1,0:T(8,128)S(1)}, u32[]{:S(2)}, u32[]{:S(2)}) collective-permute-start(f32[128,256]{1,0:T(8,128)S(1)} %slice.33), channel_id=1, source_target_pairs={{0,2},{1,3},{2,4},{3,5},{4,6},{5,7},{6,0},{7,1},{8,10},{9,11},{10,... | collective-permute-start | bytes 393224 | tf_op jit(solution)/shard_map/ppermute | solution.py:25
  52.8 34.6 %collective-permute-start.9 = (f32[128,256]{1,0:T(8,128)S(1)}, f32[128,256]{1,0:T(8,128)S(1)}, u32[]{:S(2)}, u32[]{:S(2)}) collective-permute-start(f32[128,256]{1,0:T(8,128)S(1)} %slice.32), channel_id=1, source_target_pairs={{0,6},{1,7},{2,0},{3,1},{4,2},{5,3},{6,4},{7,5},{8,14},{9,15},{10,... | collective-permute-start | bytes 393224 | tf_op jit(solution)/shard_map/ppermute | solution.py:25
  56.0 29.4 %collective-permute-start.5 = (f32[256,256]{1,0:T(8,128)}, f32[256,256]{1,0:T(8,128)S(1)}, u32[]{:S(2)}, u32[]{:S(2)}) collective-permute-start(f32[256,256]{1,0:T(8,128)} %collective-permute-done.4), channel_id=1, source_target_pairs={{0,1},{1,2},{2,3},{3,4},{4,5},{5,6},{6,7},{7,0},{8,9},{9,10},{10,1... | collective-permute-start | bytes 786440 | tf_op jit(solution)/shard_map/ppermute | solution.py:25
  59.3 28.1 %collective-permute-start.8 = (f32[256,256]{1,0:T(8,128)}, f32[256,256]{1,0:T(8,128)S(1)}, u32[]{:S(2)}, u32[]{:S(2)}) collective-permute-start(f32[256,256]{1,0:T(8,128)} %collective-permute-done.7), channel_id=1, source_target_pairs={{0,7},{1,0},{2,1},{3,2},{4,3},{5,4},{6,5},{7,6},{8,15},{9,8},{10,9... | collective-permute-start | bytes 786440 | tf_op jit(solution)/shard_map/ppermute | solution.py:25
  91.4 5.6 %collective-permute-start.11 = (f32[768,128]{1,0:T(8,128)}, f32[768,128]{1,0:T(8,128)S(1)}, u32[]{:S(2)}, u32[]{:S(2)}) collective-permute-start(f32[768,128]{1,0:T(8,128)} %pad_maximum_fusion), channel_id=1, source_target_pairs={{0,8},{8,0},{1,9},{9,1},{2,10},{10,2},{3,11},{11,3},{4,12},{12,4},... | collective-permute-start | bytes 1179656 | tf_op jit(solution)/shard_map/ppermute | solution.py:71
  118.8 24.9 %copy-start = (f32[2,256,256]{2,1,0:T(8,128)S(1)}, f32[2,256,256]{2,1,0:T(8,128)}, u32[]{:S(2)}) copy-start(f32[2,256,256]{2,1,0:T(8,128)} %broadcast_select_fusion) | copy-start | bytes 1572868

commit v3 on v2

v3 whole, which is shorter than its diff:
```python
import jax
import jax.numpy as jnp
from jax import lax
from jax.experimental import pallas as pl
from jax.experimental.pallas import tpu as pltpu
from jax.sharding import Mesh, PartitionSpec as P

PLANE = ("x", "y")
TN = (((0,), (0,)), ((), ()))
NN = (((1,), (0,)), ((), ()))
VMEM = pl.BlockSpec(memory_space=pltpu.VMEM)
LIMIT = 16 * 1024 * 1024
SMEM = pl.BlockSpec(memory_space=pltpu.SMEM)


def parts(value):
    high = value.astype(jnp.bfloat16)
    return high, (value - high.astype(jnp.float32)).astype(jnp.bfloat16)


def product(left, right, dims):
    def one(a, b):
        return lax.dot_general(a, b, dims, preferred_element_type=jnp.float32)

    return one(left[0], right[0]) + (one(left[0], right[1]) + one(left[1], right[0]))


def quarters(where_ref, chunks):
    slot, lead = where_ref[0], where_ref[1]
    for k in range(4):
        near = chunks[k][...]
        far = chunks[k + 4][...] if k else jnp.concatenate([chunks[4][...], chunks[8][...]])
        place = lax.rem(slot + k, 8)
        row = pl.multiple_of(lax.rem(place, 4) * 256, 256)
        yield row, jnp.where(place < 4, 0, 1) == lead, near, far


def cross_kernel(where_ref, *refs):
    chunks, cross_ref = refs[:9], refs[9]
    for k, (row, leads, near, far) in enumerate(quarters(where_ref, chunks)):
        term = product(parts(jnp.where(leads, far, near)), parts(jnp.where(leads, near, far)), TN)
        if k == 0:
            cross_ref[...] = term
        else:
            cross_ref[...] += term


def products_kernel(where_ref, cross_ref, *refs):
    chunks, (tiles_ref, other_ref, mine_ref, total_ref) = refs[:9], refs[9:]
    for k, (row, leads, near, far) in enumerate(quarters(where_ref, chunks)):
        tile = parts(tiles_ref[pl.ds(row, 256), :])
        for at, panel in enumerate((jnp.where(leads, near, far), jnp.where(leads, far, near))):
            term = product(parts(panel), tile, TN)
            if k == 0:
                total_ref[at] = term
            else:
                total_ref[at] += term
    mine = where_ref[2]
    for ref, half in ((other_ref, 1 - mine), (mine_ref, mine)):
        lanes = pl.ds(pl.multiple_of(half * 128, 128), 128)
        for at in range(2):
            ref[pl.ds(at * 256, 256), :] = total_ref[at, :, lanes]
        ref[pl.ds(512, 256), :] = cross_ref[:, lanes]


def update_kernel(where_ref, *refs):
    chunks, (tiles_ref, total_ref, factors_ref, out_ref) = refs[:9], refs[9:]
    upper = lax.broadcasted_iota(jnp.int32, (256, 256), 0) <= lax.broadcasted_iota(jnp.int32, (256, 256), 1)
    first, second = (parts(jnp.where(upper, factors_ref[at], 0.0)) for at in range(2))
    lead_coeff = product(first, parts(total_ref[0:256]), NN)
    lead_parts = parts(lead_coeff)
    trail = total_ref[256:512] - product(parts(total_ref[512:768]), lead_parts, NN)
    trail_parts = parts(product(second, parts(trail), NN))
    for row, leads, near, far in quarters(where_ref, chunks):
        lead = parts(jnp.where(leads, near, far))
        trail = parts(jnp.where(leads, far, near))
        change = product(lead, lead_parts, NN) + product(trail, trail_parts, NN)
        out_ref[pl.ds(row, 256), :] = tiles_ref[pl.ds(row, 256), :] - change


def products(where, chunks, tiles):
    cross = pl.pallas_call(
        cross_kernel,
        out_shape=jax.ShapeDtypeStruct((256, 256), jnp.float32),
        in_specs=[SMEM] + [VMEM] * 9,
        out_specs=VMEM,
        cost_estimate=pl.CostEstimate(flops=14_000_000_000, bytes_accessed=2300000, transcendentals=0),
        compiler_params=pltpu.CompilerParams(vmem_limit_bytes=LIMIT),
        name="cross",
    )(where, *chunks)
    half = jax.ShapeDtypeStruct((768, 128), jnp.float32)
    return pl.pallas_call(
        products_kernel,
        out_shape=(half, half),
        in_specs=[SMEM] + [VMEM] * 11,
        out_specs=(VMEM, VMEM),
        scratch_shapes=[pltpu.VMEM((2, 256, 256), jnp.float32)],
        cost_estimate=pl.CostEstimate(flops=800000000, bytes_accessed=4000000, transcendentals=0),
        compiler_params=pltpu.CompilerParams(vmem_limit_bytes=LIMIT),
        name="products",
    )(where, cross, *chunks, tiles)


def update(where, chunks, tiles, total, factors):
    return pl.pallas_call(
        update_kernel,
        out_shape=jax.ShapeDtypeStruct(tiles.shape, jnp.float32),
        in_specs=[SMEM] + [VMEM] * 12,
        out_specs=VMEM,
        cost_estimate=pl.CostEstimate(flops=1000000000, bytes_accessed=5000000, transcendentals=0),
        compiler_params=pltpu.CompilerParams(vmem_limit_bytes=LIMIT),
        name="update",
    )(where, *chunks, tiles, total, factors)


def shift(value, by):
    count = lax.axis_size("z")
    return lax.ppermute(value, "z", [(slot, (slot + by) % count) for slot in range(count)])


def owner_quarters(local):
    quarter = local.shape[0] // 4
    last = lax.axis_index("z") == lax.axis_size("z") - 1
    starts = [jnp.where(last, (3 - step) * quarter, step * quarter) for step in range(4)]
    return [lax.dynamic_slice_in_dim(local, start, quarter) for start in starts]


def scatter_quarters(pieces):
    slot = lax.axis_index("z")
    last = lax.axis_size("z") - 1
    chunk = pieces[0]
    for step in range(1, 4):
        piece = lax.ppermute(pieces[step], "z", [(0, step), (last, last - step)])
        chunk = jnp.where((slot == step) | (slot == last - step), piece, chunk)
    return chunk


def gather_panels(chunk):
    rows = chunk.shape[0]
    before2, after2 = shift(chunk, 2), shift(chunk, -2)
    before1, after1 = shift(chunk, 1), shift(chunk, -1)
    after3, before3 = shift(after2, -1), shift(before2, 1)
    upper, lower = shift(after2[: rows // 2], -2), shift(before2[rows // 2 :], 2)
    return [chunk, after1, after2, after3, upper, before3, before2, before1, lower]


def reduce_rows(other, mine):
    part = mine + lax.ppermute(other, "c", [(0, 1), (1, 0)])
    rows, columns = part.shape
    planes = lax.axis_size("x") * lax.axis_size("y")
    pieces = part.reshape(planes, rows // planes, columns)
    pieces = lax.all_to_all(pieces, PLANE, split_axis=0, concat_axis=0, tiled=True)
    pieces = jnp.broadcast_to(pieces.sum(0)[None], pieces.shape)
    pieces = lax.all_to_all(pieces, PLANE, split_axis=0, concat_axis=0, tiled=True)
    return lax.all_gather(pieces.reshape(rows, columns), "c", axis=1, tiled=True)


def per_device(eigvecs, panels, tfactors, owners):
    chunk = scatter_quarters(owner_quarters(panels[0]))
    where = jnp.stack([lax.axis_index("z"), jnp.where(owners[0] == 0, 0, 1), lax.axis_index("c")]).astype(jnp.int32)
    count = lax.axis_size("z")
    tiles = eigvecs.reshape(eigvecs.shape[0], count, -1).swapaxes(0, 1)
    chunk, tiles, where = lax.optimization_barrier((chunk, tiles, where))
    tiles = lax.all_to_all(tiles, "z", split_axis=0, concat_axis=0, tiled=True)
    tiles = tiles.reshape(-1, tiles.shape[2])
    chunks = gather_panels(chunk)
    total = reduce_rows(*products(where, chunks, tiles))
    return update(where, chunks, tiles, total, tfactors)


def solution(mesh):
    split = Mesh(mesh.devices.reshape(4, 8, 2, 8), ("x", "y", "c", "z"))
    rows = ("x", "y", "c")
    placed = (P(rows + ("z",), None), P("z", rows, None), P(), P())
    return jax.shard_map(per_device, mesh=split, in_specs=placed, out_specs=P(rows, "z"), check_vma=False)
```

time: 147 us -> 144 us (0.980); the launches traced: 147 us -> 142 us
  matrix products: 9.29 us -> 0 us
  starting transfers between devices: 48.9 us -> 55.1 us
  Pallas kernels: 0 us -> 6.18 us
  local copies, waits for them, and re-layouts: 8.46 us -> 3.03 us
    all_to_all x1, starting transfers between devices: 3.57 us -> 14.4 us  [per_device(): tiles = lax.all_to_all(tiles, 'z', split_axis=0, concat_axis=0, tiled=True)]
    dot_general x11 -> x0, matrix products: 9.29 us -> none  [dot(): lax.dot_general(left, right, (dims, ((), ())), precision=lax.Precision.HI...]
    pallas_call x0 -> x3, Pallas kernels: none -> 6.18 us  [the longest x1 3.3 us: update(): pl.pallas_call(update_kernel, out_shape=jax.ShapeDtypeStruct(tiles.shape,...]
    ppermute x8, starting transfers between devices: 30.5 us -> 26.2 us  [shift(): lax.ppermute(value, 'z', [(slot, (slot + by) % count) for slot in range(c...]
    dynamic_update_slice x7 -> x0, local copies, waits for them, and re-layouts: 3.97 us -> none  [the longest x4 1.99 us: gather_panels(): both = lax.dynamic_update_index_in_dim(both, piece, (slot - by) % 8, 0)]
    ppermute x3, waiting for transfers between devices: 10.1 us -> 6.86 us  [scatter_quarters(): piece = lax.ppermute(pieces[step], 'z', [(0, step), (last, last - step)])]
    ppermute x3, starting transfers between devices: 12.5 us -> 9.81 us  [scatter_quarters(): piece = lax.ppermute(pieces[step], 'z', [(0, step), (last, last - step)])]
    ppermute x1, starting transfers between devices: 2.41 us -> 4.61 us  [reduce_rows(): part = mine + lax.ppermute(other, 'c', [(0, 1), (1, 0)])]
  transfers between devices with their start and end apart: 13 -> 13, of which waited for: 3 -> 5; matrix products, arithmetic and copies ran while one was open for 8% -> 1% of each run, Pallas kernels for 0% -> 1%
where the time goes in v3:
time: 144 us; the launch traced here: 142 us
  starting transfers between devices  55.1 us (38%)
  blocking collectives  46.2 us (32%)
  waiting for transfers between devices  30.2 us (21%)
  Pallas kernels  6.18 us (4%)
  local copies, waits for them, and re-layouts  3.03 us (2%)
    all_to_all x2, blocking collectives, reduce_rows(): lax.all_to_all(pieces, PLANE, split_axis=0, concat_axis=0, tiled=True)  39.4 us
    ppermute x8, starting transfers between devices, shift(): lax.ppermute(value, 'z', [(slot, (slot + by) % count) for slot in range(c...  26.2 us
    ppermute x8, waiting for transfers between devices, shift(): lax.ppermute(value, 'z', [(slot, (slot + by) % count) for slot in range(c...  22 us
    all_to_all x1, starting transfers between devices, per_device(): tiles = lax.all_to_all(tiles, 'z', split_axis=0, concat_axis=0, tiled=True)  14.4 us
    ppermute x3, starting transfers between devices, scatter_quarters(): piece = lax.ppermute(pieces[step], 'z', [(0, step), (last, last - step)])  9.81 us
    ppermute x3, waiting for transfers between devices, scatter_quarters(): piece = lax.ppermute(pieces[step], 'z', [(0, step), (last, last - step)])  6.86 us
    all_gather x1, blocking collectives, reduce_rows(): lax.all_gather(pieces.reshape(rows, columns), 'c', axis=1, tiled=True)  6.75 us
    ppermute x1, starting transfers between devices, reduce_rows(): part = mine + lax.ppermute(other, 'c', [(0, 1), (1, 0)])  4.61 us
  transfers between devices with their start and end apart: 13, of which 5 were waited for; matrix products, arithmetic and copies ran while one was open for 1% of the time, Pallas kernels for 1%

profile of v3, /device:TPU:1, one launch (start us, length us, event | category | flops | bytes accessed | tf_op | source)
XLA Modules:
  0.0 142.1 jit_solution(11857085383958177612)
XLA Ops:
  0.0 1.2 dynamic-slice_bitcast_fusion
  1.3 4.8 %collective-permute-start.2 = (f32[256,256]{1,0:T(8,128)S(1)}, f32[256,256]{1,0:T(8,128)S(1)}, u32[]{:S(2)}, u32[]{:S(2)}) collective-permute-start(f32[256,256]{1,0:T(8,128)S(1)} %get-tuple-element.15), channel_id=1, source_target_pairs={{0,1},{7,6},{8,9},{15,14},{16,17},{23,22},{24,25},{31,30},{32,33},... | collective-permute-start | bytes 786440 | tf_op jit(solution)/shard_map/ppermute | solution.py:133
  6.1 2.5 %collective-permute-start.1 = (f32[256,256]{1,0:T(8,128)S(1)}, f32[256,256]{1,0:T(8,128)S(1)}, u32[]{:S(2)}, u32[]{:S(2)}) collective-permute-start(f32[256,256]{1,0:T(8,128)S(1)} %get-tuple-element.16), channel_id=1, source_target_pairs={{0,2},{7,5},{8,10},{15,13},{16,18},{23,21},{24,26},{31,29},{32,34}... | collective-permute-start | bytes 786440 | tf_op jit(solution)/shard_map/ppermute | solution.py:133
  8.6 2.5 %collective-permute-start = (f32[256,256]{1,0:T(8,128)S(1)}, f32[256,256]{1,0:T(8,128)S(1)}, u32[]{:S(2)}, u32[]{:S(2)}) collective-permute-start(f32[256,256]{1,0:T(8,128)S(1)} %get-tuple-element.17), channel_id=1, source_target_pairs={{0,3},{7,4},{8,11},{15,12},{16,19},{23,20},{24,27},{31,28},{32,35}... | collective-permute-start | bytes 786440 | tf_op jit(solution)/shard_map/ppermute | solution.py:133
  11.1 1.1 copy.8
  12.2 0.7 copy-done.2
  12.9 0.1 pad_add_fusion.where_ref
  13.0 1.2 collective-permute-done.1
  14.2 5.6 %collective-permute-done = f32[256,256]{1,0:T(8,128)S(1)} collective-permute-done((f32[256,256]{1,0:T(8,128)S(1)}, f32[256,256]{1,0:T(8,128)S(1)}, u32[]{:S(2)}, u32[]{:S(2)}) %collective-permute-start) | collective-permute-done | bytes 262176 | tf_op jit(solution)/shard_map/ppermute | solution.py:133
  19.8 1.0 fusion.1.refs_0_
  20.9 1.9 %collective-permute-start.7 = (f32[256,256]{1,0:T(8,128)S(1)}, f32[256,256]{1,0:T(8,128)S(1)}, u32[]{:S(2)}, u32[]{:S(2)}) collective-permute-start(f32[256,256]{1,0:T(8,128)S(1)} %fusion.1.refs_0_), channel_id=1, source_target_pairs={{0,2},{1,3},{2,4},{3,5},{4,6},{5,7},{6,0},{7,1},{8,10},{9,11},{10,... | collective-permute-start | bytes 786440 | tf_op jit(solution)/shard_map/ppermute | solution.py:118
  22.8 5.5 %collective-permute-start.4 = (f32[256,256]{1,0:T(8,128)S(1)}, f32[256,256]{1,0:T(8,128)S(1)}, u32[]{:S(2)}, u32[]{:S(2)}) collective-permute-start(f32[256,256]{1,0:T(8,128)S(1)} %fusion.1.refs_0_), channel_id=1, source_target_pairs={{0,6},{1,7},{2,0},{3,1},{4,2},{5,3},{6,4},{7,5},{8,14},{9,15},{10,... | collective-permute-start | bytes 786440 | tf_op jit(solution)/shard_map/ppermute | solution.py:118
  28.3 14.4 %all-to-all-start = ((f32[8,128,256]{2,1,0:T(8,128)}), f32[8,128,256]{2,1,0:T(8,128)S(1)}, u32[]{:S(2)}, u32[]{:S(2)}) async-start(f32[8,128,256]{2,1,0:T(8,128)} %bitcast.23), calls=%async_computation | async-start | bytes 2097152 | tf_op jit(solution)/shard_map/all_to_all | solution.py:164
  42.6 3.4 %collective-permute-start.9 = (f32[256,256]{1,0:T(8,128)S(1)}, f32[256,256]{1,0:T(8,128)S(1)}, u32[]{:S(2)}, u32[]{:S(2)}) collective-permute-start(f32[256,256]{1,0:T(8,128)S(1)} %fusion.1.refs_0_), channel_id=1, source_target_pairs={{0,1},{1,2},{2,3},{3,4},{4,5},{5,6},{6,7},{7,0},{8,9},{9,10},{10,1... | collective-permute-start | bytes 786440 | tf_op jit(solution)/shard_map/ppermute | solution.py:118
  46.0 3.1 %collective-permute-start.3 = (f32[256,256]{1,0:T(8,128)S(1)}, f32[256,256]{1,0:T(8,128)S(1)}, u32[]{:S(2)}, u32[]{:S(2)}) collective-permute-start(f32[256,256]{1,0:T(8,128)S(1)} %fusion.1.refs_0_), channel_id=1, source_target_pairs={{0,7},{1,0},{2,1},{3,2},{4,3},{5,4},{6,5},{7,6},{8,15},{9,8},{10,9... | collective-permute-start | bytes 786440 | tf_op jit(solution)/shard_map/ppermute | solution.py:118
  49.2 2.1 %collective-permute-start.8 = (f32[256,256]{1,0:T(8,128)S(1)}, f32[256,256]{1,0:T(8,128)S(1)}, u32[]{:S(2)}, u32[]{:S(2)}) collective-permute-start(f32[256,256]{1,0:T(8,128)S(1)} %collective-permute-done.7.refs_6_), channel_id=1, source_target_pairs={{0,1},{1,2},{2,3},{3,4},{4,5},{5,6},{6,7},{7,0},{8,9},{9,10},{10,1... | collective-permute-start | bytes 786440 | tf_op jit(solution)/shard_map/ppermute | solution.py:118
  51.3 0.0 collective-permute-done.4.refs_2_
  51.3 4.3 %collective-permute-start.5 = (f32[256,256]{1,0:T(8,128)S(1)}, f32[256,256]{1,0:T(8,128)S(1)}, u32[]{:S(2)}, u32[]{:S(2)}) collective-permute-start(f32[256,256]{1,0:T(8,128)S(1)} %collective-permute-done.4.refs_2_), channel_id=1, source_target_pairs={{0,7},{1,0},{2,1},{3,2},{4,3},{5,4},{6,5},{7,6},{8,15},{9,8},{10,9... | collective-permute-start | bytes 786440 | tf_op jit(solution)/shard_map/ppermute | solution.py:118
  55.7 2.5 %collective-permute-start.10 = (f32[128,256]{1,0:T(8,128)S(1)}, f32[128,256]{1,0:T(8,128)S(1)}, u32[]{:S(2)}, u32[]{:S(2)}) collective-permute-start(f32[128,256]{1,0:T(8,128)S(1)} %slice.13), channel_id=1, source_target_pairs={{0,2},{1,3},{2,4},{3,5},{4,6},{5,7},{6,0},{7,1},{8,10},{9,11},{10,... | collective-permute-start | bytes 393224 | tf_op jit(solution)/shard_map/ppermute | solution.py:118
  58.2 15.6 %collective-permute-done.9.refs_7_ = f32[256,256]{1,0:T(8,128)S(1)} collective-permute-done((f32[256,256]{1,0:T(8,128)S(1)}, f32[256,256]{1,0:T(8,128)S(1)}, u32[]{:S(2)}, u32[]{:S(2)}) %collective-permute-start.9) | collective-permute-done | bytes 262176 | tf_op jit(solution)/shard_map/ppermute | solution.py:118
  73.8 3.4 %collective-permute-start.6 = (f32[128,256]{1,0:T(8,128)S(1)}, f32[128,256]{1,0:T(8,128)S(1)}, u32[]{:S(2)}, u32[]{:S(2)}) collective-permute-start(f32[128,256]{1,0:T(8,128)S(1)} %slice.12), channel_id=1, source_target_pairs={{0,6},{1,7},{2,0},{3,1},{4,2},{5,3},{6,4},{7,5},{8,14},{9,15},{10,... | collective-permute-start | bytes 393224 | tf_op jit(solution)/shard_map/ppermute | solution.py:118
  77.2 0.0 collective-permute-done.3.refs_1_
  77.2 6.4 %collective-permute-done.10.refs_8_ = f32[128,256]{1,0:T(8,128)S(1)} collective-permute-done((f32[128,256]{1,0:T(8,128)S(1)}, f32[128,256]{1,0:T(8,128)S(1)}, u32[]{:S(2)}, u32[]{:S(2)}) %collective-permute-start.10) | collective-permute-done | bytes 131104 | tf_op jit(solution)/shard_map/ppermute | solution.py:118
  83.6 1.2 cross.1.cross_ref
  84.8 1.6 %products.1 = (f32[768,128]{1,0:T(8,128)S(1)}, f32[768,128]{1,0:T(8,128)S(1)}) custom-call(s32[3]{0:T(128)S(1)} %pad_add_fusion.where_ref, f32[256,256]{1,0:T(8,128)S(1)} %cross.1.cross_ref, f32[256,256]{1,0:T(8,128)S(1)} %fusion.1.refs_0_, f32[256,256]{1,0:T(8,128)S(1)} %collective-permute-done.3.refs_1_, f32[256,256]{1,0:T(8,128)S(1)} %collective-permute-done.4.refs_2_, ...), custom_call_target="tpu_custom_call" | custom-call | flops 800000000 | bytes 4000000 | tf_op jit(solution)/shard_map/products/pallas_call | solution.py:92
  86.5 4.6 %collective-permute-start.11 = (f32[768,128]{1,0:T(8,128)S(1)}, f32[768,128]{1,0:T(8,128)S(1)}, u32[]{:S(2)}, u32[]{:S(2)}) collective-permute-start(f32[768,128]{1,0:T(8,128)S(1)} %get-tuple-element.14), channel_id=1, source_target_pairs={{0,8},{8,0},{1,9},{9,1},{2,10},{10,2},{3,11},{11,3},{4,12},{12,4},... | collective-permute-start | bytes 1179656 | tf_op jit(solution)/shard_map/ppermute | solution.py:148
  91.1 1.3 collective-permute-done.11
  92.4 0.1 add.2
  92.5 21.3 %all_to_all.15 = f32[32,24,128]{2,1,0:T(8,128)S(1)} all-to-all(f32[32,24,128]{2,1,0:T(8,128)S(1)} %bitcast.27), channel_id=1, replica_groups=mesh['x'=4,'y'=8,'c'=2,'z'=8] {'x','y'}, dimensions={0} | all-to-all | bytes 786432 | tf_op jit(solution)/shard_map/all_to_all | solution.py:152
  113.8 18.2 %all_to_all.16 = f32[32,24,128]{2,1,0:T(8,128)S(1)} all-to-all(f32[32,24,128]{2,1,0:T(8,128)S(1)} %broadcast_in_dim.2), channel_id=1, replica_groups=mesh['x'=4,'y'=8,'c'=2,'z'=8] {'x','y'}, dimensions={0} | all-to-all | bytes 786432 | tf_op jit(solution)/shard_map/all_to_all | solution.py:154
  132.0 6.8 %all_gather.3.refs_10_ = f32[768,256]{1,0:T(8,128)S(1)} all-gather(f32[768,128]{1,0:T(8,128)S(1)} %bitcast.28), channel_id=1, replica_groups=mesh['x'=4,'y'=8,'c'=2,'z'=8] {'c'}, dimensions={1}, use_global_device_ids=true | all-gather | bytes 1179648 | tf_op jit(solution)/shard_map/all_gather | solution.py:155
  138.7 3.3 %update.1 = f32[1024,256]{1,0:T(8,128)} custom-call(s32[3]{0:T(128)S(1)} %pad_add_fusion.where_ref, f32[256,256]{1,0:T(8,128)S(1)} %fusion.1.refs_0_, f32[256,256]{1,0:T(8,128)S(1)} %collective-permute-done.3.refs_1_, f32[256,256]{1,0:T(8,128)S(1)} %collective-permute-done.4.refs_2_, f32[256,256]{1,0:T(8,128)S(1)} %collective-permute-done.5.refs_3_, ...), custom_call_target="tpu_custom_call" | custom-call | flops 1000000000 | bytes 5000000 | tf_op jit(solution)/shard_map/update/pallas_call | solution.py:105
  (15 shorter events, 0.1 us)
Async XLA Ops:
  0.0 11.1 %copy-start.1 = (f32[128,2048]{1,0:T(8,128)S(1)}, f32[128,2048]{1,0:T(8,128)}, u32[]{:S(2)}) copy-start(f32[128,2048]{1,0:T(8,128)} %param.4) | copy-start | bytes 3145732
  1.3 11.7 %collective-permute-start.2 = (f32[256,256]{1,0:T(8,128)S(1)}, f32[256,256]{1,0:T(8,128)S(1)}, u32[]{:S(2)}, u32[]{:S(2)}) collective-permute-start(f32[256,256]{1,0:T(8,128)S(1)} %get-tuple-element.15), channel_id=1, source_target_pairs={{0,1},{7,6},{8,9},{15,14},{16,17},{23,22},{24,25},{31,30},{32,33},... | collective-permute-start | bytes 786440 | tf_op jit(solution)/shard_map/ppermute | solution.py:133
  6.1 8.1 %collective-permute-start.1 = (f32[256,256]{1,0:T(8,128)S(1)}, f32[256,256]{1,0:T(8,128)S(1)}, u32[]{:S(2)}, u32[]{:S(2)}) collective-permute-start(f32[256,256]{1,0:T(8,128)S(1)} %get-tuple-element.16), channel_id=1, source_target_pairs={{0,2},{7,5},{8,10},{15,13},{16,18},{23,21},{24,26},{31,29},{32,34}... | collective-permute-start | bytes 786440 | tf_op jit(solution)/shard_map/ppermute | solution.py:133
  8.6 11.2 %collective-permute-start = (f32[256,256]{1,0:T(8,128)S(1)}, f32[256,256]{1,0:T(8,128)S(1)}, u32[]{:S(2)}, u32[]{:S(2)}) collective-permute-start(f32[256,256]{1,0:T(8,128)S(1)} %get-tuple-element.17), channel_id=1, source_target_pairs={{0,3},{7,4},{8,11},{15,12},{16,19},{23,20},{24,27},{31,28},{32,35}... | collective-permute-start | bytes 786440 | tf_op jit(solution)/shard_map/ppermute | solution.py:133
  12.2 0.7 copy-start.2
  20.9 28.3 %collective-permute-start.7 = (f32[256,256]{1,0:T(8,128)S(1)}, f32[256,256]{1,0:T(8,128)S(1)}, u32[]{:S(2)}, u32[]{:S(2)}) collective-permute-start(f32[256,256]{1,0:T(8,128)S(1)} %fusion.1.refs_0_), channel_id=1, source_target_pairs={{0,2},{1,3},{2,4},{3,5},{4,6},{5,7},{6,0},{7,1},{8,10},{9,11},{10,... | collective-permute-start | bytes 786440 | tf_op jit(solution)/shard_map/ppermute | solution.py:118
  22.8 28.5 %collective-permute-start.4 = (f32[256,256]{1,0:T(8,128)S(1)}, f32[256,256]{1,0:T(8,128)S(1)}, u32[]{:S(2)}, u32[]{:S(2)}) collective-permute-start(f32[256,256]{1,0:T(8,128)S(1)} %fusion.1.refs_0_), channel_id=1, source_target_pairs={{0,6},{1,7},{2,0},{3,1},{4,2},{5,3},{6,4},{7,5},{8,14},{9,15},{10,... | collective-permute-start | bytes 786440 | tf_op jit(solution)/shard_map/ppermute | solution.py:118
  28.3 56.6 %all-to-all-start = ((f32[8,128,256]{2,1,0:T(8,128)}), f32[8,128,256]{2,1,0:T(8,128)S(1)}, u32[]{:S(2)}, u32[]{:S(2)}) async-start(f32[8,128,256]{2,1,0:T(8,128)} %bitcast.23), calls=%async_computation | async-start | bytes 2097152 | tf_op jit(solution)/shard_map/all_to_all | solution.py:164
  42.6 31.1 %collective-permute-start.9 = (f32[256,256]{1,0:T(8,128)S(1)}, f32[256,256]{1,0:T(8,128)S(1)}, u32[]{:S(2)}, u32[]{:S(2)}) collective-permute-start(f32[256,256]{1,0:T(8,128)S(1)} %fusion.1.refs_0_), channel_id=1, source_target_pairs={{0,1},{1,2},{2,3},{3,4},{4,5},{5,6},{6,7},{7,0},{8,9},{9,10},{10,1... | collective-permute-start | bytes 786440 | tf_op jit(solution)/shard_map/ppermute | solution.py:118
  46.0 31.2 %collective-permute-start.3 = (f32[256,256]{1,0:T(8,128)S(1)}, f32[256,256]{1,0:T(8,128)S(1)}, u32[]{:S(2)}, u32[]{:S(2)}) collective-permute-start(f32[256,256]{1,0:T(8,128)S(1)} %fusion.1.refs_0_), channel_id=1, source_target_pairs={{0,7},{1,0},{2,1},{3,2},{4,3},{5,4},{6,5},{7,6},{8,15},{9,8},{10,9... | collective-permute-start | bytes 786440 | tf_op jit(solution)/shard_map/ppermute | solution.py:118
  49.2 34.4 %collective-permute-start.8 = (f32[256,256]{1,0:T(8,128)S(1)}, f32[256,256]{1,0:T(8,128)S(1)}, u32[]{:S(2)}, u32[]{:S(2)}) collective-permute-start(f32[256,256]{1,0:T(8,128)S(1)} %collective-permute-done.7.refs_6_), channel_id=1, source_target_pairs={{0,1},{1,2},{2,3},{3,4},{4,5},{5,6},{6,7},{7,0},{8,9},{9,10},{10,1... | collective-permute-start | bytes 786440 | tf_op jit(solution)/shard_map/ppermute | solution.py:118
  51.3 32.2 %collective-permute-start.5 = (f32[256,256]{1,0:T(8,128)S(1)}, f32[256,256]{1,0:T(8,128)S(1)}, u32[]{:S(2)}, u32[]{:S(2)}) collective-permute-start(f32[256,256]{1,0:T(8,128)S(1)} %collective-permute-done.4.refs_2_), channel_id=1, source_target_pairs={{0,7},{1,0},{2,1},{3,2},{4,3},{5,4},{6,5},{7,6},{8,15},{9,8},{10,9... | collective-permute-start | bytes 786440 | tf_op jit(solution)/shard_map/ppermute | solution.py:118
  55.7 27.9 %collective-permute-start.10 = (f32[128,256]{1,0:T(8,128)S(1)}, f32[128,256]{1,0:T(8,128)S(1)}, u32[]{:S(2)}, u32[]{:S(2)}) collective-permute-start(f32[128,256]{1,0:T(8,128)S(1)} %slice.13), channel_id=1, source_target_pairs={{0,2},{1,3},{2,4},{3,5},{4,6},{5,7},{6,0},{7,1},{8,10},{9,11},{10,... | collective-permute-start | bytes 393224 | tf_op jit(solution)/shard_map/ppermute | solution.py:118
  73.8 9.8 %collective-permute-start.6 = (f32[128,256]{1,0:T(8,128)S(1)}, f32[128,256]{1,0:T(8,128)S(1)}, u32[]{:S(2)}, u32[]{:S(2)}) collective-permute-start(f32[128,256]{1,0:T(8,128)S(1)} %slice.12), channel_id=1, source_target_pairs={{0,6},{1,7},{2,0},{3,1},{4,2},{5,3},{6,4},{7,5},{8,14},{9,15},{10,... | collective-permute-start | bytes 393224 | tf_op jit(solution)/shard_map/ppermute | solution.py:118
  86.5 5.9 %collective-permute-start.11 = (f32[768,128]{1,0:T(8,128)S(1)}, f32[768,128]{1,0:T(8,128)S(1)}, u32[]{:S(2)}, u32[]{:S(2)}) collective-permute-start(f32[768,128]{1,0:T(8,128)S(1)} %get-tuple-element.14), channel_id=1, source_target_pairs={{0,8},{8,0},{1,9},{9,1},{2,10},{10,2},{3,11},{11,3},{4,12},{12,4},... | collective-permute-start | bytes 1179656 | tf_op jit(solution)/shard_map/ppermute | solution.py:148
  132.0 6.8 %copy-start = (f32[2,256,256]{2,1,0:T(8,128)S(1)}, f32[2,256,256]{2,1,0:T(8,128)}, u32[]{:S(2)}) copy-start(f32[2,256,256]{2,1,0:T(8,128)} %refs_11_.1) | copy-start | bytes 1572868
